TPU v7x, 32 devices: a whole 2x2x4 slice. The times are simulated.
32 devices in a mesh: groups: 1, orient: 8 (over z, core), cls: 4 (over y, x).
Axes of the slice: x: 2, y: 2, z: 4, core: 2. Of those that a mesh axis runs over, the one named last changes fastest.
Arguments:
- particles: bfloat16 [384, 33024], P(('groups', 'orient', 'cls')), may hold values from -300 to 300
- projections: bfloat16 [8, 8, 33024], P('cls', 'orient')
- ctf: bfloat16 [8, 16512], replicated, may hold values from -1 to 1
- defocus_group: int32 [384], P(('groups', 'orient', 'cls')), may hold values from 0 to 7
- offsets: int32 [384, 2], P(('groups', 'orient', 'cls')), may hold values from -8 to 8
- routes: int32 [384, 4], P(('groups', 'orient', 'cls')), may hold values from 0 to 7, all different within a row; in each aligned block of 12 rows (0 to 11, 12 to 23, ...) at most 6 rows name the same one
Outputs:
- log_evidence: float32 [384], P(('groups', 'orient', 'cls'))
- data_sum: bfloat16 [8, 8, 33024], P(('groups', 'cls'), 'orient')
Inputs may be any that keep to these rules, and one draw needn't show every extreme that they name: `routes`: the 4 blocks of a particle differ; among the particles of one device no block is listed more than 6 times, and some block is listed exactly 6 times.
All inputs are finite; a program needn't handle non-finite values.
Results may differ from a plain program's by a relative error of at most 0.01.
The roundings to bfloat16 on the way count: a program that leaves them out, or rounds other values in their place, can miss the bound.
Values may be sent and summed in bfloat16 or wider, within the bound.
No kernel may reach another device: no remote copies, remote signals or barrier semaphores. Data moves between devices by JAX's collectives and lax.ppermute only.
A program may use at most 64 MiB of HBM per device.

v0:
```python
import math
import jax
import jax.numpy as jnp
import numpy as np
from jax import lax
from jax.sharding import PartitionSpec as P

KX = 86
KY = 192
BOX = 256
two_pi = 2.0 * math.pi
highest = lax.Precision.HIGHEST
local_across = np.array([0, 1, -1, 0, 0], dtype=np.int32)
local_down = np.array([0, 0, 0, 1, -1], dtype=np.int32)


def frequencies():
    column = jnp.arange(KX * KY, dtype=jnp.int32)
    return (column // KY, column % KY - KY // 2)


def rotation(shift_across, shift_down, freq_across, freq_down):
    turns = jnp.mod(freq_across * shift_across + freq_down * shift_down, BOX)
    angle = turns.astype(jnp.float32) * (two_pi / BOX)
    return (jnp.cos(angle), jnp.sin(angle))


def combine_stats(peaks, masses):
    top_value = jnp.max(peaks, axis=-1, keepdims=True)
    return top_value[..., 0] + jnp.log(jnp.sum(masses * jnp.exp(peaks - top_value), axis=-1))


def align_images(images, ctf_rows, shifts, freq_across, freq_down, pixel_count):
    real_part = images[:, :pixel_count].astype(jnp.float32)
    imag_part = images[:, pixel_count:].astype(jnp.float32)
    cos_base, sin_base = rotation(
        shifts[:, 0:1], shifts[:, 1:2], freq_across[None, :], freq_down[None, :]
    )
    first = (real_part * cos_base + imag_part * sin_base) * ctf_rows
    second = (imag_part * cos_base - real_part * sin_base) * ctf_rows
    return jnp.concatenate([first, second], axis=1).astype(jnp.bfloat16)


def spread_phase(table, ndim_rest):
    return table.reshape((table.shape[0],) + (1,) * ndim_rest + (table.shape[1],))


def turn_refs(ref_block, cos_shift, sin_shift, pixel_count):
    real_ref = ref_block[..., :pixel_count].astype(jnp.float32)
    imag_ref = ref_block[..., pixel_count:].astype(jnp.float32)
    cos_wide = spread_phase(cos_shift, real_ref.ndim - 1)
    sin_wide = spread_phase(sin_shift, real_ref.ndim - 1)
    first = real_ref[None] * cos_wide - imag_ref[None] * sin_wide
    second = real_ref[None] * sin_wide + imag_ref[None] * cos_wide
    turned = jnp.concatenate([first, second], axis=-1).astype(jnp.bfloat16)
    return (turned, real_ref * real_ref + imag_ref * imag_ref)


def back_rotate(summed, cos_shift, sin_shift, pixel_count):
    cos_wide = spread_phase(cos_shift, summed.ndim - 2)
    sin_wide = spread_phase(sin_shift, summed.ndim - 2)
    real_sum = summed[..., :pixel_count]
    imag_sum = summed[..., pixel_count:]
    first = jnp.sum(real_sum * cos_wide + imag_sum * sin_wide, axis=0)
    second = jnp.sum(imag_sum * cos_wide - real_sum * sin_wide, axis=0)
    return jnp.concatenate([first, second], axis=-1)


def slot_places(route_rows, orient_size):
    targets = route_rows.reshape(-1)
    onehot = (targets[:, None] == jnp.arange(orient_size, dtype=jnp.int32)[None, :]).astype(
        jnp.int32
    )
    before = jnp.cumsum(onehot, axis=0) - onehot
    return (targets, jnp.sum(before * onehot, axis=1))


def per_device(particles, projections, ctf, defocus_group, offsets, routes):
    pixel_count = KX * KY
    own_count = particles.shape[0]
    route_count = routes.shape[1]
    class_local = projections.shape[0]
    directions = projections.shape[1]
    group_count = ctf.shape[0]
    orient_size = lax.axis_size("orient")
    capacity = max(2, (own_count * route_count + orient_size - 1) // orient_size)
    total_slots = orient_size * capacity
    freq_across, freq_down = frequencies()
    ctf_table = ctf.astype(jnp.float32)
    group_onehot = (
        defocus_group[:, None] == jnp.arange(group_count, dtype=jnp.int32)[None, :]
    ).astype(jnp.float32)
    ctf_rows = jnp.dot(group_onehot, ctf_table, precision=highest)
    aligned = align_images(particles, ctf_rows, offsets, freq_across, freq_down, pixel_count)
    targets, orders = slot_places(routes, orient_size)
    slot_ids = targets * capacity + orders
    matches = (slot_ids[None, :] == jnp.arange(total_slots, dtype=jnp.int32)[:, None]).astype(
        jnp.int32
    )
    picked = jnp.sum(matches.reshape(total_slots, own_count, route_count), axis=2)
    send_images = jnp.dot(picked.astype(jnp.bfloat16), aligned, preferred_element_type=jnp.float32)
    send_images = send_images.astype(jnp.bfloat16).reshape(orient_size, capacity, 2 * pixel_count)
    send_codes = jnp.sum(picked * (defocus_group + 1)[None, :], axis=1).reshape(
        orient_size, capacity
    )
    tiles, codes = (
        lax.all_to_all(send_images, "orient", split_axis=0, concat_axis=0, tiled=True),
        lax.all_to_all(send_codes, "orient", split_axis=0, concat_axis=0, tiled=True),
    )
    rows_in = tiles.reshape(total_slots, 2 * pixel_count)
    codes_in = codes.reshape(total_slots)
    slot_groups = (
        codes_in[:, None] - 1 == jnp.arange(group_count, dtype=jnp.int32)[None, :]
    ).astype(jnp.float32)
    occupied = codes_in > 0
    cos_shift, sin_shift = rotation(
        jnp.asarray(local_across, dtype=jnp.int32)[:, None],
        jnp.asarray(local_down, dtype=jnp.int32)[:, None],
        freq_across[None, :],
        freq_down[None, :],
    )
    shift_total = cos_shift.shape[0]
    ctf_square = ctf_table * ctf_table
    ref_piece = lax.all_gather(projections, "cls", axis=0, tiled=True)
    piece_rows = ref_piece.shape[0]
    group_size = 2
    grouped = ref_piece.reshape(piece_rows // group_size, group_size, directions, 2 * pixel_count)

    def one_group(ref_block):
        turned, magnitude = turn_refs(ref_block, cos_shift, sin_shift, pixel_count)
        products = lax.dot_general(
            rows_in,
            turned.reshape(-1, 2 * pixel_count),
            (((1,), (1,)), ((), ())),
            preferred_element_type=jnp.float32,
        )
        energy = lax.dot_general(
            ctf_square,
            magnitude.reshape(group_size * directions, pixel_count),
            (((1,), (1,)), ((), ())),
            precision=highest,
        )
        slot_energy = jnp.dot(slot_groups, energy, precision=highest).reshape(
            total_slots, 1, group_size, directions
        )
        return (
            products.reshape(total_slots, shift_total, group_size, directions) - 0.5 * slot_energy
        )

    stacked = lax.map(one_group, grouped)
    scores = jnp.transpose(stacked, (1, 2, 0, 3, 4)).reshape(
        total_slots, shift_total, piece_rows, directions
    )
    slot_peak = jnp.max(scores, axis=(1, 2, 3))
    slot_mass = jnp.sum(jnp.exp(scores - slot_peak[:, None, None, None]), axis=(1, 2, 3))
    back_peak, back_mass = (
        lax.all_to_all(
            slot_peak.reshape(orient_size, capacity),
            "orient",
            split_axis=0,
            concat_axis=0,
            tiled=True,
        ),
        lax.all_to_all(
            slot_mass.reshape(orient_size, capacity),
            "orient",
            split_axis=0,
            concat_axis=0,
            tiled=True,
        ),
    )
    match_table = matches.astype(jnp.float32)
    entry_peak = jnp.dot(back_peak.reshape(-1), match_table, precision=highest).reshape(
        own_count, route_count
    )
    entry_mass = jnp.dot(back_mass.reshape(-1), match_table, precision=highest).reshape(
        own_count, route_count
    )
    log_evidence = combine_stats(entry_peak, entry_mass)
    slot_value = jnp.dot(picked.astype(jnp.float32), log_evidence, precision=highest).reshape(
        orient_size, capacity
    )
    evidence_in = lax.all_to_all(
        slot_value, "orient", split_axis=0, concat_axis=0, tiled=True
    ).reshape(total_slots)
    live = occupied[:, None, None, None]
    exponent = jnp.where(live, scores - evidence_in[:, None, None, None], 0.0)
    weights = jnp.where(live, jnp.exp(exponent), 0.0).astype(jnp.bfloat16)
    class_group_size = 2

    def one_group(group_index):
        weight_part = lax.dynamic_slice_in_dim(
            weights, group_index * class_group_size, class_group_size, 2
        )
        summed = lax.dot_general(
            weight_part.reshape(total_slots, -1),
            rows_in,
            (((0,), (0,)), ((), ())),
            preferred_element_type=jnp.float32,
        )
        summed = summed.reshape(shift_total, class_group_size, directions, 2 * pixel_count)
        return back_rotate(summed, cos_shift, sin_shift, pixel_count)

    results = lax.map(
        one_group,
        jnp.arange(class_local * lax.axis_size("cls") // class_group_size, dtype=jnp.int32),
    )
    data_sum = lax.psum_scatter(
        results.reshape(class_local * lax.axis_size("cls"), directions, 2 * pixel_count).astype(
            jnp.bfloat16
        ),
        "cls",
        scatter_dimension=0,
        tiled=True,
    )
    return (log_evidence, data_sum)


def solution(mesh):
    placed = (
        P(("groups", "orient", "cls"), None),
        P("cls", "orient", None),
        P(),
        P(("groups", "orient", "cls")),
        P(("groups", "orient", "cls"), None),
        P(("groups", "orient", "cls"), None),
    )
    return jax.shard_map(
        per_device,
        mesh=mesh,
        in_specs=placed,
        out_specs=(P(("groups", "orient", "cls")), P(("groups", "cls"), "orient", None)),
        check_vma=False,
    )
```

profile of v0, /device:TPU:0, one launch (start us, length us, event | category | flops | bytes accessed | tf_op | source)
XLA Modules:
  0.0 305.0 jit_solution(8616529737925251293)
XLA Ops:
  10.0 6.4 %all-to-all-start.1 = ((s32[8,1,6]{2,1,0:T(1,128)}), s32[8,1,6]{2,1,0:T(1,128)S(1)}, u32[]{:S(2)}, u32[]{:S(2)}) async-start(s32[8,1,6]{2,1,0:T(1,128)} %bitcast.3), calls=%async_computation.1 | async-start | bytes 8192 | tf_op jit(solution)/shard_map/all_to_all | solution.py:108
  17.8 6.1 %fusion.38 = (bf16[12,16512]{1,0:T(8,128)(2,1)S(1)}, bf16[12,16512]{1,0:T(8,128)(2,1)S(1)}) fusion(s32[12]{0:T(128)S(1)} %get-tuple-element.313, s32[16512]{0:T(1024)} %get-tuple-element.493, s32[12]{0:T(128)S(1)} %get-tuple-element.312, s32[16512]{0:T(1024)} %get-tuple-element.491, bf16[12,33024]{1,0:T(8,128)(2,1)} %param.12, bf16[8,16512]{1,0:T(8,128)(2,1)} %param.14, ...), kind=kOutput, calls=%fused_computation.63 | convolution fusion | flops 8718432 | bytes 1981584 | tf_op jit(solution)/shard_map/dot_general | solution.py:93
  27.5 5.2 %all-to-all-start = ((bf16[8,6,33024]{2,1,0:T(8,128)(2,1)}), bf16[8,6,33024]{2,1,0:T(8,128)(2,1)}, u32[]{:S(2)}, u32[]{:S(2)}) async-start(bf16[8,6,33024]{2,1,0:T(8,128)(2,1)} %reshape.281), calls=%async_computation | async-start | bytes 8454144 | tf_op jit(solution)/shard_map/all_to_all | solution.py:107
  33.0 15.3 %all_gather.3 = bf16[8,1,33024]{2,1,0:T(2,128)(2,1)S(1)} all-gather(bf16[2,1,33024]{2,1,0:T(2,128)(2,1)S(1)} %copy.39), channel_id=1, replica_groups=mesh['groups'=1,'orient'=8,'cls'=4] {'cls'}, dimensions={0}, use_global_device_ids=true | all-gather | bytes 660480 | tf_op jit(solution)/shard_map/all_gather | solution.py:124
  48.2 3.2 %reduce.6 = bf16[8,33024]{1,0:T(8,128)(2,1)S(1)} reduce(bf16[8,1,33024]{2,1,0:T(2,128)(2,1)S(1)} %all_gather.3, bf16[]{:T(256)} %constant.106), dimensions={1}, to_apply=%all_gather.3.reduce_sub_computation | reduce | bytes 1056770 | tf_op jit(solution)/shard_map/all_gather | solution.py:124
  53.4 74.1 %all-to-all-done = bf16[8,6,33024]{2,1,0:T(8,128)(2,1)} async-done(((bf16[8,6,33024]{2,1,0:T(8,128)(2,1)}), bf16[8,6,33024]{2,1,0:T(8,128)(2,1)}, u32[]{:S(2)}, u32[]{:S(2)}) %all-to-all-start) | async-done | bytes 3170336 | tf_op jit(solution)/shard_map/all_to_all | solution.py:107
  130.4 57.9 %while.24 = (s32[]{:T(128)}, f32[4,48,5,2,1]{1,3,2,4,0:T(2,128)S(1)}, bf16[4,2,1,33024]{3,1,2,0:T(2,128)(2,1)}, bf16[48,33024]{1,0:T(8,128)(2,1)S(1)}, f32[8,165...) while((s32[]{:T(128)}, ...), condition=%wide.region_5.6_spmd.clone.clone, body=%wide.region_4.5_spmd.clone.clone.sunk | while | flops 39077952 | bytes 9925141 | solution.py:150
  130.4 3.1 %fusion.95 = (f32[5,16512]{1,0:T(8,128)S(1)}, f32[5,16512]{1,0:T(8,128)S(1)}) fusion(s32[5]{0:T(128)S(1)} %get-tuple-element.481, s32[16512]{0:T(1024)} %get-tuple-element.482, s32[5]{0:T(128)S(1)} %get-tuple-element.479, s32[16512]{0:T(1024)} %get-tuple-element.480), kind=kLoop, calls=%fused_computation.20.clone.1 | loop fusion | flops 1320960 | bytes 792616 | tf_op jit(solution)/shard_map/cos | solution.py:25
  144.9 3.1 %fusion.95 = (f32[5,16512]{1,0:T(8,128)S(1)}, f32[5,16512]{1,0:T(8,128)S(1)}) fusion(s32[5]{0:T(128)S(1)} %get-tuple-element.481, s32[16512]{0:T(1024)} %get-tuple-element.482, s32[5]{0:T(128)S(1)} %get-tuple-element.479, s32[16512]{0:T(1024)} %get-tuple-element.480), kind=kLoop, calls=%fused_computation.20.clone.1 | loop fusion | flops 1320960 | bytes 792616 | tf_op jit(solution)/shard_map/cos | solution.py:25
  159.4 3.1 %fusion.95 = (f32[5,16512]{1,0:T(8,128)S(1)}, f32[5,16512]{1,0:T(8,128)S(1)}) fusion(s32[5]{0:T(128)S(1)} %get-tuple-element.481, s32[16512]{0:T(1024)} %get-tuple-element.482, s32[5]{0:T(128)S(1)} %get-tuple-element.479, s32[16512]{0:T(1024)} %get-tuple-element.480), kind=kLoop, calls=%fused_computation.20.clone.1 | loop fusion | flops 1320960 | bytes 792616 | tf_op jit(solution)/shard_map/cos | solution.py:25
  173.8 3.1 %fusion.95 = (f32[5,16512]{1,0:T(8,128)S(1)}, f32[5,16512]{1,0:T(8,128)S(1)}) fusion(s32[5]{0:T(128)S(1)} %get-tuple-element.481, s32[16512]{0:T(1024)} %get-tuple-element.482, s32[5]{0:T(128)S(1)} %get-tuple-element.479, s32[16512]{0:T(1024)} %get-tuple-element.480), kind=kLoop, calls=%fused_computation.20.clone.1 | loop fusion | flops 1320960 | bytes 792616 | tf_op jit(solution)/shard_map/cos | solution.py:25
  189.1 3.3 %all-to-all-start.3 = ((f32[8,1,6]{2,1,0:T(1,128)}), f32[8,1,6]{2,1,0:T(1,128)S(1)}, u32[]{:S(2)}, u32[]{:S(2)}) async-start(f32[8,1,6]{2,1,0:T(1,128)} %bitcast.8), calls=%async_computation.3 | async-start | bytes 8192 | tf_op jit(solution)/shard_map/all_to_all | solution.py:164
  193.2 4.7 %all-to-all-done.3 = f32[8,1,6]{2,1,0:T(1,128)S(1)} async-done(((f32[8,1,6]{2,1,0:T(1,128)}), f32[8,1,6]{2,1,0:T(1,128)S(1)}, u32[]{:S(2)}, u32[]{:S(2)}) %all-to-all-start.3) | async-done | bytes 224 | tf_op jit(solution)/shard_map/all_to_all | solution.py:164
  197.9 3.3 %all-to-all-start.2 = ((f32[8,1,6]{2,1,0:T(1,128)}), f32[8,1,6]{2,1,0:T(1,128)S(1)}, u32[]{:S(2)}, u32[]{:S(2)}) async-start(f32[8,1,6]{2,1,0:T(1,128)} %bitcast.4), calls=%async_computation.2 | async-start | bytes 8192 | tf_op jit(solution)/shard_map/all_to_all | solution.py:157
  202.5 4.2 %all-to-all-done.2 = f32[8,1,6]{2,1,0:T(1,128)S(1)} async-done(((f32[8,1,6]{2,1,0:T(1,128)}), f32[8,1,6]{2,1,0:T(1,128)S(1)}, u32[]{:S(2)}, u32[]{:S(2)}) %all-to-all-start.2) | async-done | bytes 224 | tf_op jit(solution)/shard_map/all_to_all | solution.py:157
  209.0 3.3 %all-to-all-start.4 = ((f32[8,1,6]{2,1,0:T(1,128)}), f32[8,1,6]{2,1,0:T(1,128)S(1)}, u32[]{:S(2)}, u32[]{:S(2)}) async-start(f32[8,1,6]{2,1,0:T(1,128)} %bitcast.13), calls=%async_computation.4 | async-start | bytes 8192 | tf_op jit(solution)/shard_map/all_to_all | solution.py:183
  212.7 5.0 %all-to-all-done.4 = f32[8,1,6]{2,1,0:T(1,128)S(1)} async-done(((f32[8,1,6]{2,1,0:T(1,128)}), f32[8,1,6]{2,1,0:T(1,128)S(1)}, u32[]{:S(2)}, u32[]{:S(2)}) %all-to-all-start.4) | async-done | bytes 224 | tf_op jit(solution)/shard_map/all_to_all | solution.py:183
  218.6 28.0 %while.25 = (s32[]{:T(128)}, bf16[4,2,1,33024]{3,2,1,0:T(2,128)(2,1)}, s32[4]{0:T(128)S(1)}, bf16[48,5,8,1]{0,2,1,3:T(8,128)(2,1)S(1)}, bf16[48,33024]{1,0:T(8,1...) while((s32[]{:T(128)}, ...), condition=%wide.region_13.14_spmd.clone.clone, body=%wide.region_10.13_spmd.clone.clone.sunk | while | flops 34543108 | bytes 8065315 | solution.py:204
  220.4 3.1 %fusion.100 = (f32[5,16512]{1,0:T(8,128)S(1)}, f32[5,16512]{1,0:T(8,128)S(1)}) fusion(s32[5]{0:T(128)S(1)} %get-tuple-element.518, s32[16512]{0:T(1024)} %get-tuple-element.519, s32[5]{0:T(128)S(1)} %get-tuple-element.516, s32[16512]{0:T(1024)} %get-tuple-element.517), kind=kLoop, calls=%fused_computation.47.clone.1 | loop fusion | flops 1320960 | bytes 792616 | tf_op jit(solution)/shard_map/cos | solution.py:25
  227.4 3.1 %fusion.100 = (f32[5,16512]{1,0:T(8,128)S(1)}, f32[5,16512]{1,0:T(8,128)S(1)}) fusion(s32[5]{0:T(128)S(1)} %get-tuple-element.518, s32[16512]{0:T(1024)} %get-tuple-element.519, s32[5]{0:T(128)S(1)} %get-tuple-element.516, s32[16512]{0:T(1024)} %get-tuple-element.517), kind=kLoop, calls=%fused_computation.47.clone.1 | loop fusion | flops 1320960 | bytes 792616 | tf_op jit(solution)/shard_map/cos | solution.py:25
  234.4 3.1 %fusion.100 = (f32[5,16512]{1,0:T(8,128)S(1)}, f32[5,16512]{1,0:T(8,128)S(1)}) fusion(s32[5]{0:T(128)S(1)} %get-tuple-element.518, s32[16512]{0:T(1024)} %get-tuple-element.519, s32[5]{0:T(128)S(1)} %get-tuple-element.516, s32[16512]{0:T(1024)} %get-tuple-element.517), kind=kLoop, calls=%fused_computation.47.clone.1 | loop fusion | flops 1320960 | bytes 792616 | tf_op jit(solution)/shard_map/cos | solution.py:25
  241.4 3.1 %fusion.100 = (f32[5,16512]{1,0:T(8,128)S(1)}, f32[5,16512]{1,0:T(8,128)S(1)}) fusion(s32[5]{0:T(128)S(1)} %get-tuple-element.518, s32[16512]{0:T(1024)} %get-tuple-element.519, s32[5]{0:T(128)S(1)} %get-tuple-element.516, s32[16512]{0:T(1024)} %get-tuple-element.517), kind=kLoop, calls=%fused_computation.47.clone.1 | loop fusion | flops 1320960 | bytes 792616 | tf_op jit(solution)/shard_map/cos | solution.py:25
  246.6 4.8 %convert_reduce_fusion = bf16[4,2,33024]{2,1,0:T(2,128)(2,1)S(1)} fusion(bf16[4,2,1,33024]{3,2,1,0:T(2,128)(2,1)} %get-tuple-element.82), kind=kLoop, calls=%fused_computation.73 | loop fusion | bytes 1056768 | tf_op jit(solution)/shard_map/convert_element_type | solution.py:209
  253.7 42.7 %all-reduce.3.cloned.1.call-done = bf16[8,1,33024]{2,0,1:T(8,128)(2,1)} async-done(((bf16[8,1,33024]{2,0,1:T(8,128)(2,1)}), bf16[8,1,33024]{2,0,1:T(8,128)(2,1)}) %all-reduce.3.cloned.1.call-update) | async-done | bytes 528400
  (157 shorter events, 80.9 us)
Async XLA Ops:
  10.0 17.5 %all-to-all-start.1 = ((s32[8,1,6]{2,1,0:T(1,128)}), s32[8,1,6]{2,1,0:T(1,128)S(1)}, u32[]{:S(2)}, u32[]{:S(2)}) async-start(s32[8,1,6]{2,1,0:T(1,128)} %bitcast.3), calls=%async_computation.1 | async-start | bytes 8192 | tf_op jit(solution)/shard_map/all_to_all | solution.py:108
  27.5 5.2 %copy-start.3 = (bf16[2,1,33024]{2,0,1:T(2,128)(2,1)S(1)}, bf16[2,1,33024]{2,0,1:T(2,128)(2,1)}, u32[]{:S(2)}) copy-start(bf16[2,1,33024]{2,0,1:T(2,128)(2,1)} %param.13) | copy-start | bytes 396292
  27.5 100.0 %all-to-all-start = ((bf16[8,6,33024]{2,1,0:T(8,128)(2,1)}), bf16[8,6,33024]{2,1,0:T(8,128)(2,1)}, u32[]{:S(2)}, u32[]{:S(2)}) async-start(bf16[8,6,33024]{2,1,0:T(8,128)(2,1)} %reshape.281), calls=%async_computation | async-start | bytes 8454144 | tf_op jit(solution)/shard_map/all_to_all | solution.py:107
  48.2 4.2 %copy-start.2 = (bf16[8,16512]{1,0:T(8,128)(2,1)S(1)}, bf16[8,16512]{1,0:T(8,128)(2,1)}, u32[]{:S(2)}) copy-start(bf16[8,16512]{1,0:T(8,128)(2,1)} %param.14) | copy-start | bytes 792580
  53.4 77.0 %copy-start.4 = (s32[5]{0:T(128)S(1)}, s32[5]{0:T(128)}, u32[]{:S(2)}) copy-start(s32[5]{0:T(128)} %constant.95.clone) | copy-start | bytes 64
  53.4 77.0 %copy-start.5 = (s32[5]{0:T(128)S(1)}, s32[5]{0:T(128)}, u32[]{:S(2)}) copy-start(s32[5]{0:T(128)} %constant.96.clone) | copy-start | bytes 64
  134.5 0.7 copy-start
  140.1 2.2 copy-start.1
  149.0 0.7 copy-start
  154.6 2.2 copy-start.1
  163.5 0.7 copy-start
  169.1 2.2 copy-start.1
  177.9 0.7 copy-start
  183.6 2.2 copy-start.1
  189.1 8.9 %all-to-all-start.3 = ((f32[8,1,6]{2,1,0:T(1,128)}), f32[8,1,6]{2,1,0:T(1,128)S(1)}, u32[]{:S(2)}, u32[]{:S(2)}) async-start(f32[8,1,6]{2,1,0:T(1,128)} %bitcast.8), calls=%async_computation.3 | async-start | bytes 8192 | tf_op jit(solution)/shard_map/all_to_all | solution.py:164
  197.9 8.8 %all-to-all-start.2 = ((f32[8,1,6]{2,1,0:T(1,128)}), f32[8,1,6]{2,1,0:T(1,128)S(1)}, u32[]{:S(2)}, u32[]{:S(2)}) async-start(f32[8,1,6]{2,1,0:T(1,128)} %bitcast.4), calls=%async_computation.2 | async-start | bytes 8192 | tf_op jit(solution)/shard_map/all_to_all | solution.py:157
  208.2 10.4 %copy-start.6 = (f32[12]{0:T(128)}, f32[12]{0:T(128)S(1)}, u32[]{:S(2)}) copy-start(f32[12]{0:T(128)S(1)} %log_add_fusion) | copy-start | bytes 148
  209.0 8.8 %all-to-all-start.4 = ((f32[8,1,6]{2,1,0:T(1,128)}), f32[8,1,6]{2,1,0:T(1,128)S(1)}, u32[]{:S(2)}, u32[]{:S(2)}) async-start(f32[8,1,6]{2,1,0:T(1,128)} %bitcast.13), calls=%async_computation.4 | async-start | bytes 8192 | tf_op jit(solution)/shard_map/all_to_all | solution.py:183
  212.3 84.0 %all-reduce.3.cloned.1.call-start = ((), (), s32[]{:S(2)}) async-start(), calls=%async_computation.5 | async-start | bytes 1056768
  251.4 1.1 copy-start.7
Sparse Core Ops, SparseCore 0:
  252.5 43.7 all-reduce.2
where the time goes:
time: 307 us; the launch traced here: 305 us
  waiting for transfers between devices  131 us (43%)
  other arithmetic  46.6 us (15%)
  local copies, waits for them, and re-layouts  44 us (14%)
  matrix products  28.7 us (9%)
  starting transfers between devices  21.8 us (7%)
  blocking collectives  15.3 us (5%)
  between operations  14.9 us (5%)
    all_to_all x1, waiting for transfers between devices, per_device(): lax.all_to_all(send_images, 'orient', split_axis=0, concat_axis=0, tiled=...  74.1 us
    unnamed x2, waiting for transfers between devices  42.7 us
    cos x8, other arithmetic, rotation(): return (jnp.cos(angle), jnp.sin(angle))  24.6 us
    all_gather x1, blocking collectives, per_device(): ref_piece = lax.all_gather(projections, 'cls', axis=0, tiled=True)  15.3 us
    dot_general x4, matrix products, one_group(): lax.dot_general(ctf_square, magnitude.reshape(group_size * directions, pi...  9.16 us
    add x4, local copies, waits for them, and re-layouts, turn_refs(): second = real_ref[None] * sin_wide + imag_ref[None] * cos_wide  9.07 us
    dot_general x4, matrix products, one_group(): lax.dot_general(rows_in, turned.reshape(-1, 2 * pixel_count), (((1,), (1,...  8.57 us
    all_to_all x1, starting transfers between devices, per_device(): lax.all_to_all(send_codes, 'orient', split_axis=0, concat_axis=0, tiled=T...  6.35 us
  transfers between devices with their start and end apart: 6, of which 5 were waited for; matrix products, arithmetic and copies ran while one was open for 6% of the time, Pallas kernels for 0%

commit v1 on v0

--- a/solution.py
+++ b/solution.py
@@ -4,6 +4,7 @@
 import numpy as np
 from jax import lax
 from jax.sharding import PartitionSpec as P
+from jax.lax import axis_index, axis_size, ppermute
 
 KX = 86
 KY = 192
@@ -121,7 +122,21 @@
     )
     shift_total = cos_shift.shape[0]
     ctf_square = ctf_table * ctf_table
-    ref_piece = lax.all_gather(projections, "cls", axis=0, tiled=True)
+    shares = axis_size("cls")
+    crops = tuple(((dev_i, (dev_i + 1) % shares) for dev_i in range(shares)))
+    nodes = tuple(((dev_i, (dev_i - 1) % shares) for dev_i in range(shares)))
+    local_next, g_now = ([projections], [projections])
+    for _ in range(shares // 2):
+        item_now = ppermute(local_next[-1], "cls", perm=crops)
+        local_next.append(item_now)
+    for _ in [*range((shares - 1) // 2)]:
+        finding = ppermute(g_now[-1], axis_name="cls", perm=nodes)
+        g_now.append(finding)
+    ref_piece = jnp.roll(
+        jnp.concatenate([*local_next[::-1], *g_now[1:]], axis=0),
+        (axis_index("cls") - shares // 2) * projections.shape[0],
+        axis=0,
+    )
     piece_rows = ref_piece.shape[0]
     group_size = 2
     grouped = ref_piece.reshape(piece_rows // group_size, group_size, directions, 2 * pixel_count)

time: 307 us -> 310 us (level)
  blocking collectives: 15.3 us -> 0 us
  waiting for transfers between devices: 131 us -> 144 us
  local copies, waits for them, and re-layouts: 44 us -> 49.4 us
  starting transfers between devices: 21.8 us -> 25.3 us
  other arithmetic: 46.6 us -> 43.4 us
    all_gather x1 -> x0, blocking collectives: 15.3 us -> none  [per_device(): ref_piece = lax.all_gather(projections, 'cls', axis=0, tiled=True)]
    all_to_all x1, waiting for transfers between devices: 74.1 us -> 87 us  [per_device(): lax.all_to_all(send_images, 'orient', split_axis=0, concat_axis=0, tiled=...]
    concatenate x0 -> x1, local copies, waits for them, and re-layouts: none -> 5.46 us  [per_device(): jnp.roll(jnp.concatenate([*local_next[::-1], *g_now[1:]], axis=0), (axis_...]
    ppermute x0 -> x3, starting transfers between devices: none -> 4.68 us  [the longest x2 3.66 us: per_device(): item_now = ppermute(local_next[-1], 'cls', perm=crops)]
    all_gather x1 -> x0, other arithmetic: 3.18 us -> none  [per_device(): ref_piece = lax.all_gather(projections, 'cls', axis=0, tiled=True)]
  transfers between devices with their start and end apart: 6 -> 9, of which waited for: 5 -> 6; matrix products, arithmetic and copies ran while one was open for 6% -> 7% of each run, Pallas kernels for 0% -> 0%
where the time goes in v1:
time: 310 us; the launch traced here: 308 us
  waiting for transfers between devices  144 us (46%)
  local copies, waits for them, and re-layouts  49.4 us (16%)
  other arithmetic  43.4 us (14%)
  matrix products  28.7 us (9%)
  starting transfers between devices  25.3 us (8%)
  between operations  14.9 us (5%)
    all_to_all x1, waiting for transfers between devices, per_device(): lax.all_to_all(send_images, 'orient', split_axis=0, concat_axis=0, tiled=...  87 us
    unnamed x2, waiting for transfers between devices  42.6 us
    cos x8, other arithmetic, rotation(): return (jnp.cos(angle), jnp.sin(angle))  24.6 us
    dot_general x4, matrix products, one_group(): lax.dot_general(ctf_square, magnitude.reshape(group_size * directions, pi...  9.16 us
    add x4, local copies, waits for them, and re-layouts, turn_refs(): second = real_ref[None] * sin_wide + imag_ref[None] * cos_wide  9.07 us
    dot_general x4, matrix products, one_group(): lax.dot_general(rows_in, turned.reshape(-1, 2 * pixel_count), (((1,), (1,...  8.57 us
  transfers between devices with their start and end apart: 9, of which 6 were waited for; matrix products, arithmetic and copies ran while one was open for 7% of the time, Pallas kernels for 0%

profile of v1, /device:TPU:0, one launch (start us, length us, event | category | flops | bytes accessed | tf_op | source)
XLA Modules:
  0.0 308.5 jit_solution(12903853699565778974)
XLA Ops:
  7.2 3.0 collective-permute-start
  14.0 5.3 %all-to-all-start.1 = ((s32[8,1,6]{2,1,0:T(1,128)}), s32[8,1,6]{2,1,0:T(1,128)S(1)}, u32[]{:S(2)}, u32[]{:S(2)}) async-start(s32[8,1,6]{2,1,0:T(1,128)} %bitcast.3), calls=%async_computation.1 | async-start | bytes 8192 | tf_op jit(solution)/shard_map/all_to_all | solution.py:109
  20.8 6.1 %fusion.38 = (bf16[12,16512]{1,0:T(8,128)(2,1)S(1)}, bf16[12,16512]{1,0:T(8,128)(2,1)S(1)}) fusion(s32[12]{0:T(128)S(1)} %get-tuple-element.313, s32[16512]{0:T(1024)} %get-tuple-element.493, s32[12]{0:T(128)S(1)} %get-tuple-element.312, s32[16512]{0:T(1024)} %get-tuple-element.491, bf16[12,33024]{1,0:T(8,128)(2,1)} %param.12, bf16[8,16512]{1,0:T(8,128)(2,1)} %param.14, ...), kind=kOutput, calls=%fused_computation.63 | convolution fusion | flops 8718432 | bytes 1981584 | tf_op jit(solution)/shard_map/dot_general | solution.py:94
  31.1 5.1 %all-to-all-start = ((bf16[8,6,33024]{2,1,0:T(8,128)(2,1)}), bf16[8,6,33024]{2,1,0:T(8,128)(2,1)}, u32[]{:S(2)}, u32[]{:S(2)}) async-start(bf16[8,6,33024]{2,1,0:T(8,128)(2,1)} %reshape.281), calls=%async_computation | async-start | bytes 8454144 | tf_op jit(solution)/shard_map/all_to_all | solution.py:108
  37.4 5.5 %concatenate.20 = bf16[16,1,33024]{2,0,1:T(8,128)(2,1)S(1)} concatenate(bf16[2,1,33024]{2,0,1:T(2,128)(2,1)S(1)} %collective-permute-done.1, bf16[2,1,33024]{2,0,1:T(2,128)(2,1)S(1)} %collective-permute-done, bf16[2,1,33024]{2,0,1:T(2,128)(2,1)S(1)} %copy-done.2, bf16[2,1,33024]{2,0,1:T(2,128)(2,1)S(1)} %collective-permute-done.2, ...), dimensions={0} | concatenate | bytes 2113536 | tf_op jit(solution)/shard_map/jit(_roll_dynamic)/concatenate | solution.py:135
  44.1 87.0 %all-to-all-done = bf16[8,6,33024]{2,1,0:T(8,128)(2,1)} async-done(((bf16[8,6,33024]{2,1,0:T(8,128)(2,1)}), bf16[8,6,33024]{2,1,0:T(8,128)(2,1)}, u32[]{:S(2)}, u32[]{:S(2)}) %all-to-all-start) | async-done | bytes 3170336 | tf_op jit(solution)/shard_map/all_to_all | solution.py:108
  133.9 57.9 %while.24 = (s32[]{:T(128)}, f32[4,48,5,2,1]{1,3,2,4,0:T(2,128)S(1)}, bf16[4,2,1,33024]{3,1,2,0:T(2,128)(2,1)}, bf16[48,33024]{1,0:T(8,128)(2,1)S(1)}, f32[8,165...) while((s32[]{:T(128)}, ...), condition=%wide.region_5.6_spmd.clone.clone, body=%wide.region_4.5_spmd.clone.clone.sunk | while | flops 39077952 | bytes 9925141 | solution.py:165
  133.9 3.1 fusion.95
  148.4 3.1 fusion.95
  162.9 3.1 fusion.95
  177.3 3.1 fusion.95
  192.6 3.3 %all-to-all-start.3 = ((f32[8,1,6]{2,1,0:T(1,128)}), f32[8,1,6]{2,1,0:T(1,128)S(1)}, u32[]{:S(2)}, u32[]{:S(2)}) async-start(f32[8,1,6]{2,1,0:T(1,128)} %bitcast.8), calls=%async_computation.3 | async-start | bytes 8192 | tf_op jit(solution)/shard_map/all_to_all | solution.py:179
  196.7 4.7 %all-to-all-done.3 = f32[8,1,6]{2,1,0:T(1,128)S(1)} async-done(((f32[8,1,6]{2,1,0:T(1,128)}), f32[8,1,6]{2,1,0:T(1,128)S(1)}, u32[]{:S(2)}, u32[]{:S(2)}) %all-to-all-start.3) | async-done | bytes 224 | tf_op jit(solution)/shard_map/all_to_all | solution.py:179
  201.4 3.3 %all-to-all-start.2 = ((f32[8,1,6]{2,1,0:T(1,128)}), f32[8,1,6]{2,1,0:T(1,128)S(1)}, u32[]{:S(2)}, u32[]{:S(2)}) async-start(f32[8,1,6]{2,1,0:T(1,128)} %bitcast.4), calls=%async_computation.2 | async-start | bytes 8192 | tf_op jit(solution)/shard_map/all_to_all | solution.py:172
  206.0 4.2 %all-to-all-done.2 = f32[8,1,6]{2,1,0:T(1,128)S(1)} async-done(((f32[8,1,6]{2,1,0:T(1,128)}), f32[8,1,6]{2,1,0:T(1,128)S(1)}, u32[]{:S(2)}, u32[]{:S(2)}) %all-to-all-start.2) | async-done | bytes 224 | tf_op jit(solution)/shard_map/all_to_all | solution.py:172
  212.5 3.3 %all-to-all-start.4 = ((f32[8,1,6]{2,1,0:T(1,128)}), f32[8,1,6]{2,1,0:T(1,128)S(1)}, u32[]{:S(2)}, u32[]{:S(2)}) async-start(f32[8,1,6]{2,1,0:T(1,128)} %bitcast.13), calls=%async_computation.4 | async-start | bytes 8192 | tf_op jit(solution)/shard_map/all_to_all | solution.py:198
  216.2 5.0 %all-to-all-done.4 = f32[8,1,6]{2,1,0:T(1,128)S(1)} async-done(((f32[8,1,6]{2,1,0:T(1,128)}), f32[8,1,6]{2,1,0:T(1,128)S(1)}, u32[]{:S(2)}, u32[]{:S(2)}) %all-to-all-start.4) | async-done | bytes 224 | tf_op jit(solution)/shard_map/all_to_all | solution.py:198
  222.1 28.0 %while.25 = (s32[]{:T(128)}, bf16[4,2,1,33024]{3,2,1,0:T(2,128)(2,1)}, s32[4]{0:T(128)S(1)}, bf16[48,5,8,1]{0,2,1,3:T(8,128)(2,1)S(1)}, bf16[48,33024]{1,0:T(8,1...) while((s32[]{:T(128)}, ...), condition=%wide.region_13.14_spmd.clone.clone, body=%wide.region_10.13_spmd.clone.clone.sunk | while | flops 34543108 | bytes 8065315 | solution.py:219
  223.9 3.1 fusion.100
  230.9 3.1 fusion.100
  237.9 3.1 fusion.100
  244.9 3.1 fusion.100
  250.1 4.8 %convert_reduce_fusion = bf16[4,2,33024]{2,1,0:T(2,128)(2,1)S(1)} fusion(bf16[4,2,1,33024]{3,2,1,0:T(2,128)(2,1)} %get-tuple-element.82), kind=kLoop, calls=%fused_computation.73 | loop fusion | bytes 1056768 | tf_op jit(solution)/shard_map/convert_element_type | solution.py:224
  257.2 42.6 %all-reduce.3.cloned.1.call-done = bf16[8,1,33024]{2,0,1:T(8,128)(2,1)} async-done(((bf16[8,1,33024]{2,0,1:T(8,128)(2,1)}), bf16[8,1,33024]{2,0,1:T(8,128)(2,1)}) %all-reduce.3.cloned.1.call-update) | async-done | bytes 528400
  (162 shorter events, 82.6 us)
Async XLA Ops:
  7.2 23.3 %collective-permute-start = (bf16[2,1,33024]{2,0,1:T(2,128)(2,1)}, bf16[2,1,33024]{2,0,1:T(2,128)(2,1)S(1)}, u32[]{:S(2)}, u32[]{:S(2)}) collective-permute-start(bf16[2,1,33024]{2,0,1:T(2,128)(2,1)} %param.13), channel_id=1, source_target_pairs={{0,1},{1,2},{2,3},{3,0},{4,5},{5,6},{6,7},{7,4},{8,9},{9,10},{10,1... | collective-permute-start | bytes 396296 | tf_op jit(solution)/shard_map/ppermute | solution.py:130
  10.2 27.0 %collective-permute-start.2 = (bf16[2,1,33024]{2,0,1:T(2,128)(2,1)}, bf16[2,1,33024]{2,0,1:T(2,128)(2,1)S(1)}, u32[]{:S(2)}, u32[]{:S(2)}) collective-permute-start(bf16[2,1,33024]{2,0,1:T(2,128)(2,1)} %param.13), channel_id=1, source_target_pairs={{0,3},{1,0},{2,1},{3,2},{4,7},{5,4},{6,5},{7,6},{8,11},{9,8},{10,9... | collective-permute-start | bytes 396296 | tf_op jit(solution)/shard_map/ppermute | solution.py:133
  14.0 17.1 %all-to-all-start.1 = ((s32[8,1,6]{2,1,0:T(1,128)}), s32[8,1,6]{2,1,0:T(1,128)S(1)}, u32[]{:S(2)}, u32[]{:S(2)}) async-start(s32[8,1,6]{2,1,0:T(1,128)} %bitcast.3), calls=%async_computation.1 | async-start | bytes 8192 | tf_op jit(solution)/shard_map/all_to_all | solution.py:109
  30.5 5.8 %copy-start.3 = (bf16[8,16512]{1,0:T(8,128)(2,1)S(1)}, bf16[8,16512]{1,0:T(8,128)(2,1)}, u32[]{:S(2)}) copy-start(bf16[8,16512]{1,0:T(8,128)(2,1)} %param.14) | copy-start | bytes 792580
  30.5 6.9 %copy-start.2 = (bf16[2,1,33024]{2,0,1:T(2,128)(2,1)S(1)}, bf16[2,1,33024]{2,0,1:T(2,128)(2,1)}, u32[]{:S(2)}) copy-start(bf16[2,1,33024]{2,0,1:T(2,128)(2,1)} %param.13) | copy-start | bytes 396292
  30.5 6.9 %collective-permute-start.1 = (bf16[2,1,33024]{2,0,1:T(2,128)(2,1)S(1)}, bf16[2,1,33024]{2,0,1:T(2,128)(2,1)S(1)}, u32[]{:S(2)}, u32[]{:S(2)}) collective-permute-start(bf16[2,1,33024]{2,0,1:T(2,128)(2,1)S(1)} %collective-permute-done), channel_id=1, source_target_pairs={{0,1},{1,2},{2,3},{3,0},{4,5},{5,6},{6,7},{7,4},{8,9},{9,10},{10,1... | collective-permute-start | bytes 396296 | tf_op jit(solution)/shard_map/ppermute | solution.py:130
  31.1 99.9 %all-to-all-start = ((bf16[8,6,33024]{2,1,0:T(8,128)(2,1)}), bf16[8,6,33024]{2,1,0:T(8,128)(2,1)}, u32[]{:S(2)}, u32[]{:S(2)}) async-start(bf16[8,6,33024]{2,1,0:T(8,128)(2,1)} %reshape.281), calls=%async_computation | async-start | bytes 8454144 | tf_op jit(solution)/shard_map/all_to_all | solution.py:108
  44.0 89.8 %copy-start.4 = (s32[5]{0:T(128)S(1)}, s32[5]{0:T(128)}, u32[]{:S(2)}) copy-start(s32[5]{0:T(128)} %constant.124.clone) | copy-start | bytes 64
  44.0 89.8 %copy-start.5 = (s32[5]{0:T(128)S(1)}, s32[5]{0:T(128)}, u32[]{:S(2)}) copy-start(s32[5]{0:T(128)} %constant.125.clone) | copy-start | bytes 64
  138.0 0.7 copy-start
  143.6 2.2 copy-start.1
  152.5 0.7 copy-start
  158.1 2.2 copy-start.1
  166.9 0.7 copy-start
  172.6 2.2 copy-start.1
  181.4 0.7 copy-start
  187.1 2.2 copy-start.1
  192.6 8.9 %all-to-all-start.3 = ((f32[8,1,6]{2,1,0:T(1,128)}), f32[8,1,6]{2,1,0:T(1,128)S(1)}, u32[]{:S(2)}, u32[]{:S(2)}) async-start(f32[8,1,6]{2,1,0:T(1,128)} %bitcast.8), calls=%async_computation.3 | async-start | bytes 8192 | tf_op jit(solution)/shard_map/all_to_all | solution.py:179
  201.4 8.8 %all-to-all-start.2 = ((f32[8,1,6]{2,1,0:T(1,128)}), f32[8,1,6]{2,1,0:T(1,128)S(1)}, u32[]{:S(2)}, u32[]{:S(2)}) async-start(f32[8,1,6]{2,1,0:T(1,128)} %bitcast.4), calls=%async_computation.2 | async-start | bytes 8192 | tf_op jit(solution)/shard_map/all_to_all | solution.py:172
  211.7 10.4 %copy-start.6 = (f32[12]{0:T(128)}, f32[12]{0:T(128)S(1)}, u32[]{:S(2)}) copy-start(f32[12]{0:T(128)S(1)} %log_add_fusion) | copy-start | bytes 148
  212.5 8.8 %all-to-all-start.4 = ((f32[8,1,6]{2,1,0:T(1,128)}), f32[8,1,6]{2,1,0:T(1,128)S(1)}, u32[]{:S(2)}, u32[]{:S(2)}) async-start(f32[8,1,6]{2,1,0:T(1,128)} %bitcast.13), calls=%async_computation.4 | async-start | bytes 8192 | tf_op jit(solution)/shard_map/all_to_all | solution.py:198
  215.8 83.9 %all-reduce.3.cloned.1.call-start = ((), (), s32[]{:S(2)}) async-start(), calls=%async_computation.5 | async-start | bytes 1056768
  254.9 1.1 copy-start.7
Sparse Core Ops, SparseCore 0:
  256.0 43.7 all-reduce.2
